TPU v7x, 32 devices: a whole 2x2x4 slice. The times are simulated.
32 devices in a mesh: dp: 16 (over z, y, x), tensor: 2 (over core).
Axes of the slice: x: 2, y: 2, z: 4, core: 2. Of those that a mesh axis runs over, the one named last changes fastest.
Arguments:
- tokens: bfloat16 [32768, 768], P('dp'), may hold values from -6 to 6
- cotangent: bfloat16 [32768, 768], P('dp'), may hold values from -6 to 6
- seq_ids: int32 [32768], P('dp'), may hold values from 0 to 39, as said below
- block_slot: int32 [216], replicated, may hold values from 0 to 223, as said below
- masters: float32 [2, 224, 128, 128], P('tensor', 'dp')
- left_stats: float32 [2, 224, 128, 128], P('tensor', 'dp'), as said below
- right_stats: float32 [2, 224, 128, 128], P('tensor', 'dp'), as said below
- left_roots: float32 [2, 224, 128, 128], P('tensor', 'dp'), as said below
- right_roots: float32 [2, 224, 128, 128], P('tensor', 'dp'), as said below
- vectors: float32 [9984], replicated
- vector_momentum: float32 [9984], replicated, may hold values from -0.9 to 0.9
Outputs:
- mixed: bfloat16 [32768, 768], P(('dp', 'tensor'))
- input_grad: float32 [32768, 768], P(('dp', 'tensor'))
- matrix_grads: float32 [2, 224, 128, 128], P('tensor', 'dp')
- new_masters: float32 [2, 224, 128, 128], P('tensor', 'dp')
- new_left: float32 [2, 224, 128, 128], P('tensor', 'dp')
- new_right: float32 [2, 224, 128, 128], P('tensor', 'dp')
- new_vectors: float32 [9984], replicated
- new_vector_momentum: float32 [9984], replicated
Inputs may be any that keep to these rules, and one draw needn't show every extreme that they name: `seq_ids`: each aligned block of 2048 tokens holds either one sequence or 4 sequences of 512 tokens, half of the blocks of each kind; ids count the sequences in order from 0 and are equal within a sequence. `block_slot`: Distinct; slot s belongs to index s // 14 of dp; slots that no block names hold no block. `left_stats`: symmetric in each slot. `right_stats`: symmetric in each slot. `left_roots`: symmetric in each slot. `right_roots`: symmetric in each slot.
All inputs are finite; a program needn't handle non-finite values.
Results may differ from a plain program's by a relative error of at most 0.0095.
Values may be sent and summed in bfloat16 or wider, within the bound.
No kernel may reach another device: no remote copies, remote signals or barrier semaphores. Data moves between devices by JAX's collectives and lax.ppermute only.
A program may use at most 256 MiB of HBM per device.

v0:
```python
import jax
import jax.numpy as jnp
from jax import lax
from jax.sharding import PartitionSpec as P

H = 12
HD = 64
ROT = 16
FF = 3072
norm_eps = 1e-05
floor_score = -1e30
rate_matrix = 0.03
rate_vector = 1.5
decay_vector = 0.9


def contract(first_op, second_op, first_dim, second_dim):
    return lax.dot_general(
        first_op,
        second_op,
        (((first_dim,), (second_dim,)), ((), ())),
        preferred_element_type=jnp.float32,
    )


def unblock(blocks, row_total, col_total):
    blk_size = blocks.shape[-1]
    return (
        blocks.reshape(row_total // blk_size, col_total // blk_size, blk_size, blk_size)
        .transpose(0, 2, 1, 3)
        .reshape(row_total, col_total)
    )


def to_blocks(matrix, blk_size):
    row_count, col_count = matrix.shape
    return (
        matrix.reshape(row_count // blk_size, blk_size, col_count // blk_size, blk_size)
        .transpose(0, 2, 1, 3)
        .reshape(-1, blk_size, blk_size)
    )


def rotate(values, cosine_tab, sine_tab, local_heads):
    tok_rows = values.shape[0]
    shaped = values.reshape(tok_rows, local_heads, HD)
    rot_half = ROT // 2
    lower_half = shaped[:, :, :rot_half]
    upper_half = shaped[:, :, rot_half:ROT]
    turned = jnp.concatenate(
        [
            lower_half * cosine_tab - upper_half * sine_tab,
            upper_half * cosine_tab + lower_half * sine_tab,
            shaped[:, :, ROT:],
        ],
        axis=2,
    )
    return turned.reshape(tok_rows, local_heads * HD)


def slice_rows(array, row_start, row_count):
    return lax.dynamic_slice_in_dim(array, row_start, row_count, 0)


def back_norm(gradient, gain_vec, normed_rows, inv_rows):
    scaled = gradient * gain_vec
    centered = scaled - jnp.mean(scaled, axis=1, keepdims=True)
    return inv_rows * (
        centered - normed_rows * jnp.mean(scaled * normed_rows, axis=1, keepdims=True)
    )


def on_device(
    tokens,
    cotangent,
    seq_ids,
    block_slot,
    masters,
    left_stats,
    right_stats,
    left_roots,
    right_roots,
    vectors,
    vector_momentum,
):
    tensor_ways = lax.axis_size("tensor")
    tensor_index = lax.axis_index("tensor")
    data_ways = lax.axis_size("dp")
    data_index = lax.axis_index("dp")
    tok_rows, model_width = tokens.shape
    blk_size = masters.shape[-1]
    slot_count = masters.shape[1]
    local_heads = H // tensor_ways
    width_qkv = 3 * model_width // tensor_ways
    width_heads = model_width // tensor_ways
    width_hidden = FF // tensor_ways
    blocks_qkv = model_width // blk_size * (width_qkv // blk_size)
    blocks_attn = width_heads // blk_size * (model_width // blk_size)
    blocks_in = model_width // blk_size * (width_hidden // blk_size)
    mark_two = blocks_qkv + blocks_attn
    mark_three = mark_two + blocks_in
    copies = masters[0].astype(jnp.bfloat16)
    gathered = lax.all_gather(copies, "dp", axis=0, tiled=True)
    picked = jnp.take(gathered, block_slot, axis=0)
    w_qkv = unblock(picked[:blocks_qkv], model_width, width_qkv)
    w_attn = unblock(picked[blocks_qkv:mark_two], width_heads, model_width)
    w_in = unblock(picked[mark_two:mark_three], model_width, width_hidden)
    w_out = unblock(picked[mark_three:], width_hidden, model_width)
    gain_one = vectors[0:model_width]
    bias_one = vectors[model_width : 2 * model_width]
    gain_two = vectors[2 * model_width : 3 * model_width]
    bias_two = vectors[3 * model_width : 4 * model_width]
    bias_qkv = lax.dynamic_slice_in_dim(
        vectors, 4 * model_width + tensor_index * width_qkv, width_qkv
    )
    bias_attn = vectors[7 * model_width : 8 * model_width]
    bias_in = lax.dynamic_slice_in_dim(
        vectors, 8 * model_width + tensor_index * width_hidden, width_hidden
    )
    bias_out = vectors[8 * model_width + FF : 9 * model_width + FF]
    places = jnp.arange(tok_rows, dtype=jnp.int32)
    seq_first = jnp.concatenate([places[:1] == 0, seq_ids[1:] != seq_ids[:-1]])
    seq_start = lax.cummax(jnp.where(seq_first, places, 0), axis=0)
    position = (places - seq_start).astype(jnp.float32)
    rot_half = ROT // 2
    inverse = 10000.0 ** (-(2.0 * jnp.arange(rot_half, dtype=jnp.float32)) / ROT)
    angles = position[:, None] * inverse[None, :]
    cosine_tab = jnp.cos(angles)[:, None, :]
    sine_tab = jnp.sin(angles)[:, None, :]
    tokens_f = tokens.astype(jnp.float32)
    row_mean = jnp.mean(tokens_f, axis=1, keepdims=True)
    centered = tokens_f - row_mean
    inv_std = lax.rsqrt(jnp.mean(centered * centered, axis=1, keepdims=True) + norm_eps)
    normed = centered * inv_std
    norm_one = (normed * gain_one + bias_one).astype(jnp.bfloat16)
    norm_two = (normed * gain_two + bias_two).astype(jnp.bfloat16)
    mixed_qkv = jnp.dot(norm_one, w_qkv, preferred_element_type=jnp.float32) + bias_qkv
    queries = (
        rotate(mixed_qkv[:, :width_heads], cosine_tab, sine_tab, local_heads)
        .astype(jnp.bfloat16)
        .reshape(tok_rows, local_heads, HD)
    )
    keys_rot = (
        rotate(mixed_qkv[:, width_heads : 2 * width_heads], cosine_tab, sine_tab, local_heads)
        .astype(jnp.bfloat16)
        .reshape(tok_rows, local_heads, HD)
    )
    values_all = (
        mixed_qkv[:, 2 * width_heads :].astype(jnp.bfloat16).reshape(tok_rows, local_heads, HD)
    )
    blk_rows = min(512, tok_rows)
    block_total = tok_rows // blk_rows
    score_scale = HD ** (-0.5)

    def block_scores(block_index):
        row_low = block_index * blk_rows
        row_high = row_low + blk_rows
        scores = (
            jnp.einsum(
                "qhe,khe->hqk",
                queries[row_low:row_high],
                keys_rot[:row_high],
                preferred_element_type=jnp.float32,
            )
            * score_scale
        )
        allowed = (seq_ids[row_low:row_high, None] == seq_ids[None, :row_high]) & (
            places[row_low:row_high, None] >= places[None, :row_high]
        )
        return jnp.where(allowed[None], scores, floor_score)

    outputs = []
    log_sums = []
    for block_index in range(block_total):
        key_span = (block_index + 1) * blk_rows
        scores = block_scores(block_index)
        row_max = jnp.max(scores, axis=2, keepdims=True)
        exp_scores = jnp.exp(scores - row_max)
        row_total = jnp.sum(exp_scores, axis=2, keepdims=True)
        weights_low = (exp_scores / row_total).astype(jnp.bfloat16)
        outputs.append(
            jnp.einsum(
                "hqk,khe->qhe",
                weights_low,
                values_all[:key_span],
                preferred_element_type=jnp.float32,
            )
        )
        log_sums.append(row_max + jnp.log(row_total))
    attended = jnp.concatenate(outputs, axis=0).reshape(tok_rows, width_heads).astype(jnp.bfloat16)
    pre_hidden = jnp.dot(norm_two, w_in, preferred_element_type=jnp.float32) + bias_in
    hidden = jax.nn.gelu(pre_hidden, approximate=False).astype(jnp.bfloat16)
    own_rows = tok_rows // tensor_ways
    row_base = tensor_index * own_rows
    row_start = jnp.int32(0)
    attn_part = slice_rows(attended, row_start, lax.axis_size("tensor") * own_rows)
    hidden_part = slice_rows(hidden, row_start, lax.axis_size("tensor") * own_rows)
    branch_total = lax.psum_scatter(
        (
            jnp.dot(attn_part, w_attn, preferred_element_type=jnp.float32)
            + jnp.dot(hidden_part, w_out, preferred_element_type=jnp.float32)
        ).astype(jnp.bfloat16),
        "tensor",
        scatter_dimension=0,
        tiled=True,
    ).astype(jnp.float32)
    tokens_own = slice_rows(tokens_f, row_base, own_rows)
    mixed = (tokens_own + branch_total + bias_attn + bias_out).astype(jnp.bfloat16)
    grad_out_w = contract(hidden, cotangent, 0, 0)
    grad_hidden = contract(cotangent, w_out, 1, 1)
    density = jnp.exp(-0.5 * pre_hidden * pre_hidden) * 0.3989422804014327
    slope = 0.5 * (1.0 + lax.erf(pre_hidden * 0.7071067811865476)) + pre_hidden * density
    grad_pre = (grad_hidden * slope).astype(jnp.bfloat16)
    grad_in_w = contract(norm_two, grad_pre, 0, 0)
    grad_norm_two = contract(grad_pre, w_in, 1, 1)
    grad_bias_in = jnp.sum(grad_pre.astype(jnp.float32), axis=0)
    grad_attn_w = contract(attended, cotangent, 0, 0)
    grad_attended = (
        contract(cotangent, w_attn, 1, 1).astype(jnp.bfloat16).reshape(tok_rows, local_heads, HD)
    )
    grad_queries = []
    grad_keys = jnp.zeros((tok_rows, local_heads, HD), jnp.float32)
    grad_values = jnp.zeros((tok_rows, local_heads, HD), jnp.float32)
    for block_index in range(block_total):
        row_low = block_index * blk_rows
        row_high = row_low + blk_rows
        scores = block_scores(block_index)
        prob_full = jnp.exp(scores - log_sums[block_index])
        prob_low = prob_full.astype(jnp.bfloat16)
        grad_probs = jnp.einsum(
            "qhe,khe->hqk",
            grad_attended[row_low:row_high],
            values_all[:row_high],
            preferred_element_type=jnp.float32,
        )
        row_delta = jnp.sum(prob_full * grad_probs, axis=2, keepdims=True)
        grad_scores = (prob_full * (grad_probs - row_delta)).astype(jnp.bfloat16)
        grad_queries.append(
            jnp.einsum(
                "hqk,khe->qhe", grad_scores, keys_rot[:row_high], preferred_element_type=jnp.float32
            )
            * score_scale
        )
        grad_keys = grad_keys.at[:row_high].add(
            jnp.einsum(
                "hqk,qhe->khe",
                grad_scores,
                queries[row_low:row_high],
                preferred_element_type=jnp.float32,
            )
            * score_scale
        )
        grad_values = grad_values.at[:row_high].add(
            jnp.einsum(
                "hqk,qhe->khe",
                prob_low,
                grad_attended[row_low:row_high],
                preferred_element_type=jnp.float32,
            )
        )
    grad_query_all = jnp.concatenate(grad_queries, axis=0).reshape(tok_rows, width_heads)
    grad_mixed = jnp.concatenate(
        [
            rotate(grad_query_all, cosine_tab, -sine_tab, local_heads),
            rotate(grad_keys.reshape(tok_rows, width_heads), cosine_tab, -sine_tab, local_heads),
            grad_values.reshape(tok_rows, width_heads),
        ],
        axis=1,
    ).astype(jnp.bfloat16)
    grad_qkv_w = contract(norm_one, grad_mixed, 0, 0)
    grad_norm_one = contract(grad_mixed, w_qkv, 1, 1)
    grad_bias_qkv = jnp.sum(grad_mixed.astype(jnp.float32), axis=0)
    row_start = jnp.int32(0)
    row_count = lax.axis_size("tensor") * own_rows
    normed_rows = slice_rows(normed, row_start, row_count)
    inv_rows = slice_rows(inv_std, row_start, row_count)
    input_part = lax.psum_scatter(
        (
            back_norm(
                slice_rows(grad_norm_one, row_start, row_count), gain_one, normed_rows, inv_rows
            )
            + back_norm(
                slice_rows(grad_norm_two, row_start, row_count), gain_two, normed_rows, inv_rows
            )
        ).astype(jnp.bfloat16),
        "tensor",
        scatter_dimension=0,
        tiled=True,
    ).astype(jnp.float32)
    cot_own = slice_rows(cotangent, row_base, own_rows).astype(jnp.float32)
    input_grad = cot_own + input_part
    bias_grad_out = jnp.sum(cot_own, axis=0)
    pieces = [
        jnp.sum(grad_norm_one * normed, axis=0),
        jnp.sum(grad_norm_one, axis=0),
        jnp.sum(grad_norm_two * normed, axis=0),
        jnp.sum(grad_norm_two, axis=0),
        lax.dynamic_update_slice_in_dim(
            jnp.zeros((3 * model_width,), jnp.float32), grad_bias_qkv, tensor_index * width_qkv, 0
        ),
        bias_grad_out,
        lax.dynamic_update_slice_in_dim(
            jnp.zeros((FF,), jnp.float32), grad_bias_in, tensor_index * width_hidden, 0
        ),
        bias_grad_out,
    ]
    vector_sum = lax.psum(jnp.concatenate(pieces), ("dp", "tensor"))
    grad_scale = 1.0 / jnp.sqrt(jnp.float32(data_ways * tok_rows))
    vector_grad = vector_sum * grad_scale
    new_momentum = decay_vector * vector_momentum + (1.0 - decay_vector) * vector_grad
    new_vectors = vectors - rate_vector * new_momentum
    local_blocks = jnp.concatenate(
        [
            to_blocks(grad_qkv_w, blk_size),
            to_blocks(grad_attn_w, blk_size),
            to_blocks(grad_in_w, blk_size),
            to_blocks(grad_out_w, blk_size),
        ],
        axis=0,
    )
    slot_total = data_ways * slot_count
    summed = lax.psum(local_blocks, "dp")
    owner_of = (
        jnp.full((slot_total,), -1, jnp.int32)
        .at[block_slot]
        .set(jnp.arange(block_slot.shape[0], dtype=jnp.int32))
    )
    mine_blocks = lax.dynamic_slice_in_dim(owner_of, data_index * slot_count, slot_count, 0)
    owned = jnp.where(
        (mine_blocks >= 0)[:, None, None],
        jnp.take(summed, jnp.maximum(mine_blocks, 0), axis=0),
        0.0,
    )
    grad_blocks = owned * grad_scale
    highest = lax.Precision.HIGHEST
    new_left = (
        0.5 * left_stats[0]
        + 0.5 * jnp.einsum("sij,skj->sik", grad_blocks, grad_blocks, precision=highest) / blk_size
    )
    new_right = (
        0.5 * right_stats[0]
        + 0.5 * jnp.einsum("sji,sjk->sik", grad_blocks, grad_blocks, precision=highest) / blk_size
    )
    update_step = jnp.einsum("sij,sjk->sik", left_roots[0], grad_blocks, precision=highest)
    update_step = jnp.einsum("sij,sjk->sik", update_step, right_roots[0], precision=highest)
    new_masters = masters[0] - rate_matrix * update_step
    return (
        mixed,
        input_grad,
        grad_blocks[None],
        new_masters[None],
        new_left[None],
        new_right[None],
        new_vectors,
        new_momentum,
    )


def solution(mesh):
    return jax.shard_map(
        on_device,
        mesh=mesh,
        in_specs=(
            P("dp", None),
            P("dp", None),
            P("dp"),
            P(),
            P("tensor", "dp", None, None),
            P("tensor", "dp", None, None),
            P("tensor", "dp", None, None),
            P("tensor", "dp", None, None),
            P("tensor", "dp", None, None),
            P(),
            P(),
        ),
        out_specs=(
            P(("dp", "tensor"), None),
            P(("dp", "tensor"), None),
            P("tensor", "dp", None, None),
            P("tensor", "dp", None, None),
            P("tensor", "dp", None, None),
            P("tensor", "dp", None, None),
            P(),
            P(),
        ),
        check_vma=False,
    )
```

profile of v0, /device:TPU:0, one launch (start us, length us, event | category | flops | bytes accessed | tf_op | source)
XLA Modules:
  0.0 953.4 jit_solution(12270465933401899179)
XLA Ops:
  28.0 88.9 %all-gather.2.cloned.1.call-done = bf16[224,128,128]{2,1,0:T(8,128)(2,1)} async-done(((bf16[14,128,128]{2,1,0:T(8,128)(2,1)}), bf16[224,128,128]{2,1,0:T(8,128)(2,1)}) %all-gather.2.cloned.1.call-update) | async-done | bytes 7340048 | tf_op jit(solution)/shard_map/all_gather | solution.py:103
  116.9 11.4 %gather_fusion = bf16[216,128,128]{2,1,0:T(8,128)(2,1)} fusion(bf16[224,128,128]{2,1,0:T(8,128)(2,1)} %all-gather.2.cloned.1.call-done, s32[1024]{0:T(1024)S(1)} %pad_clamp_fusion.1), kind=kCustom, calls=%fused_computation | custom fusion | bytes 14156640 | tf_op jit(solution)/shard_map/jit(_take)/gather | solution.py:104
  194.5 7.3 multiply_convert_fusion.2
  206.2 8.4 fusion.161
  214.7 9.0 fusion.2
  223.7 10.5 %fusion.53 = f32[2048,6,64]{0,2,1:T(8,128)} fusion(f32[2048,6,64]{0,2,1:T(8,128)} %copy-done.8, bf16[512,6,64]{0,2,1:T(8,128)(2,1)S(1)} %bitcast.244, f32[6,512,1536]{2,1,0:T(8,128)} %get-tuple-element.177, f32[6,512]{1,0:T(8,128)S(1)} %log_add_fusion.1), kind=kOutput, calls=%fused_computation.109 | convolution fusion | flops 614006784 | bytes 23998464 | tf_op jit(solution)/shard_map/hqk,qhe->khe/dot_general | solution.py:254
  234.2 12.1 %multiply_reduce_fusion.1 = (f32[6,512]{1,0:T(8,128)S(1)}, f32[6,512,1536]{2,1,0:T(8,128)}) fusion(f32[6,512,1536]{2,1,0:T(8,128)} %get-tuple-element.177, f32[6,512]{1,0:T(8,128)S(1)} %log_add_fusion.1, bf16[512,6,64]{0,2,1:T(8,128)(2,1)S(1)} %bitcast.245, bf16[1536,6,64]{0,2,1:T(8,128)(2,1)S(1)} %bitcast.241), kind=kOutput, calls=%fused_computation.14 | convolution fusion | flops 618132480 | bytes 39346176 | tf_op jit(solution)/shard_map/qhe,khe->hqk/dot_general | solution.py:230
  246.3 12.9 %multiply_convert_fusion.1 = bf16[6,512,1536]{2,1,0:T(8,128)(2,1)S(1)} fusion(f32[6,512,1536]{2,1,0:T(8,128)} %get-tuple-element.187, f32[6,512,1536]{2,1,0:T(8,128)} %get-tuple-element.177, f32[6,512]{1,0:T(8,128)S(1)} %get-tuple-element.186, f32[6,512]{1,0:T(8,128)S(1)} %log_add_fusion.1), kind=kLoop, calls=%fused_computation.13 | loop fusion | flops 18874368 | bytes 47210496 | tf_op jit(solution)/shard_map/convert_element_type | solution.py:237
  265.9 34.4 %fusion.6 = (bf16[2048,1536]{1,0:T(8,128)(2,1)S(1)}, f32[2048,1536]{1,0:T(8,128)}) fusion(f32[1536]{0:T(1024)S(1)} %copy-done.66, bf16[96,8,12,128]{3,2,1,0:T(8,128)(2,1)S(1)} %bitcast.253, bf16[2048,768]{1,0:T(8,128)(2,1)S(1)} %copy-done.2, f32[768]{0:T(1024)S(1)} %copy-done.70, f32[768]{0:T(1024)S(1)} %copy-done.65, f32[2048]{0:T(1024)S(1)} %add_rsqrt_fusion, ...), kind=kOutput, calls=%fused_computation.24 | convolution fusion | flops 5048893440 | bytes 24408064 | tf_op jit(solution)/shard_map/dot_general | solution.py:191
  300.4 13.2 %convert_reduce_fusion = (f32[1536]{0:T(1024)}, bf16[2048,1536]{1,0:T(8,128)(2,1)S(1)}) fusion(f32[2048,1536]{1,0:T(8,128)} %get-tuple-element.171, f32[1536]{0:T(1024)S(1)} %copy-done.66, bf16[2048,768]{1,0:T(8,128)(2,1)S(1)} %copy-done.19, bf16[192,8,6,128]{3,2,1,0:T(8,128)(2,1)S(1)} %bitcast.255), kind=kOutput, calls=%fused_computation.32 | convolution fusion | flops 4872731136 | bytes 24391680 | tf_op jit(solution)/shard_map/dot_general | solution.py:18
  313.6 7.0 fusion.60
  327.5 10.7 %fusion.160 = (f32[6,512]{1,0:T(8,128)S(1)}, f32[6,512,2048]{2,1,0:T(8,128)}) fusion(bf16[2048,6,64]{0,2,1:T(8,128)(2,1)S(1)} %get-tuple-element.194, bf16[2048,6,64]{0,2,1:T(8,128)(2,1)S(1)} %copy-done.13, pred[512,2048]{1,0:T(8,128)(4,1)S(1)} %copy-done.17), kind=kOutput, calls=%fused_computation.283 | convolution fusion | flops 824177664 | bytes 28192768 | tf_op jit(solution)/shard_map/qhe,khe->hqk/dot_general | solution.py:159
  338.3 10.9 %fusion = f32[6,512]{1,0:T(8,128)S(1)} fusion(f32[6,512,2048]{2,1,0:T(8,128)} %get-tuple-element.175, f32[6,512]{1,0:T(8,128)S(1)} %get-tuple-element.174), kind=kLoop, calls=%fused_computation.9 | loop fusion | flops 12579840 | bytes 25190400 | tf_op jit(solution)/shard_map/reduce_sum | solution.py:179
  349.2 11.9 %fusion.39 = bf16[2048,6,64]{0,2,1:T(8,128)(2,1)} fusion(f32[2048,6,64]{0,2,1:T(8,128)S(1)} %copy-done.9, bf16[512,6,64]{0,2,1:T(8,128)(2,1)S(1)} %bitcast.242, f32[6,512,2048]{2,1,0:T(8,128)} %get-tuple-element.175, f32[6,512]{1,0:T(8,128)S(1)} %log_add_fusion), kind=kOutput, calls=%fused_computation.97 | convolution fusion | flops 819462144 | bytes 30289920 | tf_op jit(solution)/shard_map/hqk,qhe->khe/dot_general | solution.py:254
  361.1 19.5 %multiply_reduce_fusion = (f32[6,512]{1,0:T(8,128)S(1)}, f32[6,512,2048]{2,1,0:T(8,128)}) fusion(f32[6,512,2048]{2,1,0:T(8,128)} %get-tuple-element.175, f32[6,512]{1,0:T(8,128)S(1)} %log_add_fusion, bf16[512,6,64]{0,2,1:T(8,128)(2,1)S(1)} %bitcast.243, bf16[2048,6,64]{0,2,1:T(8,128)(2,1)S(1)} %bitcast.227), kind=kOutput, calls=%fused_computation.4 | convolution fusion | flops 824177664 | bytes 52322304 | tf_op jit(solution)/shard_map/qhe,khe->hqk/dot_general | solution.py:230
  380.6 16.9 %multiply_convert_fusion = bf16[6,512,2048]{2,1,0:T(8,128)(2,1)S(1)} fusion(f32[6,512,2048]{2,1,0:T(8,128)} %get-tuple-element.189, f32[6,512,2048]{2,1,0:T(8,128)} %get-tuple-element.175, f32[6,512]{1,0:T(8,128)S(1)} %get-tuple-element.188, f32[6,512]{1,0:T(8,128)S(1)} %log_add_fusion), kind=kLoop, calls=%fused_computation.3 | loop fusion | flops 25165824 | bytes 62939136 | tf_op jit(solution)/shard_map/convert_element_type | solution.py:237
  412.1 11.4 %multiply_reduce_fusion.4 = (f32[768]{0:T(1024)S(1)}, f32[2048]{0:T(1024)S(1)}, f32[2048]{0:T(1024)S(1)}, f32[768]{0:T(1024)S(1)}, f32[768]{0:T(1024)S(1)}, /*in...) fusion(bf16[2048,768]{1,0:T(8,128)(2,1)S(1)} %copy-done.3, ...), kind=kOutput, calls=%fused_computation.67 | convolution fusion | flops 3664761856 | bytes 22284288 | tf_op jit(solution)/shard_map/dot_general | solution.py:18
  430.3 9.9 %fusion.100 = bf16[6,64,512]{2,1,0:T(8,128)(2,1)S(1)} fusion(bf16[1536,6,64]{0,2,1:T(8,128)(2,1)} %bitcast.240, f32[6,512,1536]{2,1,0:T(8,128)} %get-tuple-element.177, f32[6,512]{1,0:T(8,128)S(1)} %copy-done.59, f32[6,512]{1,0:T(8,128)S(1)} %copy-done.57), kind=kOutput, calls=%fused_computation.169 | convolution fusion | flops 618332160 | bytes 20471808 | tf_op jit(solution)/shard_map/hqk,khe->qhe/dot_general | solution.py:182
  440.2 10.7 %fusion.101 = bf16[6,64,512]{2,1,0:T(8,128)(2,1)S(1)} fusion(bf16[2048,6,64]{0,2,1:T(8,128)(2,1)S(1)} %bitcast.228, f32[6,512,2048]{2,1,0:T(8,128)} %get-tuple-element.175, f32[6,512]{1,0:T(8,128)S(1)} %fusion, f32[6,512]{1,0:T(8,128)S(1)} %get-tuple-element.174), kind=kOutput, calls=%fused_computation.170 | convolution fusion | flops 824377344 | bytes 27156480 | tf_op jit(solution)/shard_map/hqk,khe->qhe/dot_general | solution.py:182
  460.3 11.8 %fusion.153 = f32[768,1536]{1,0:T(8,128)} fusion(bf16[2048,1536]{1,0:T(8,128)(2,1)} %copy-done.74, bf16[2048,768]{1,0:T(8,128)(2,1)} %param.31, f32[768]{0:T(1024)S(1)} %copy-done.71, f32[768]{0:T(1024)S(1)} %copy-done.65, f32[2048]{0:T(1024)S(1)} %add_rsqrt_fusion, f32[2048]{0:T(1024)S(1)} %broadcast_multiply_fusion.4), kind=kOutput, calls=%fused_computation.276 | convolution fusion | flops 4841275392 | bytes 14178304 | tf_op jit(solution)/shard_map/dot_general | solution.py:18
  485.4 8.7 fusion.165
  528.8 7.8 pad_maximum_fusion
  551.0 42.9 %psum.15 = f32[9984]{0:T(1024)S(1)} all-reduce(f32[9984]{0:T(1024)S(1)} %constant_dynamic-update-slice_fusion), channel_id=1, replica_groups=mesh['dp'=16,'tensor'=2] {'dp','tensor'}, use_global_device_ids=true, to_apply=%region_31.32 | all-reduce | flops 9984 | bytes 79872 | tf_op jit(solution)/shard_map/psum | solution.py:307
  598.7 329.6 %all-reduce.4.cloned.1.call-done = f32[216,128,128]{2,1,0:T(8,128)} async-done(((f32[216,128,128]{2,1,0:T(8,128)}), f32[216,128,128]{2,1,0:T(8,128)}) %all-reduce.4.cloned.1.call-update) | async-done | bytes 14155792 | tf_op jit(solution)/shard_map/psum | solution.py:322
  (307 shorter events, 219.9 us)
Async XLA Ops:
  7.2 936.1 %copy-start = (f32[1,14,128,128]{3,2,1,0:T(8,128)S(1)}, f32[1,14,128,128]{3,2,1,0:T(8,128)}, u32[]{:S(2)}) copy-start(f32[1,14,128,128]{3,2,1,0:T(8,128)} %param.38) | copy-start | bytes 2752516
  7.2 14.8 %slice-start.5 = ((s32[2048]{0:T(1024)}), s32[1024]{0:T(1024)S(1)}, s32[]{:S(2)}) async-start(s32[2048]{0:T(1024)} %param.33), calls=%async_computation.11 | async-start | bytes 8192 | tf_op jit(solution)/shard_map/slice | solution.py:167
  7.2 17.1 %copy-start.53 = (s32[2048]{0:T(1024)S(1)}, s32[2048]{0:T(1024)}, u32[]{:S(2)}) copy-start(s32[2048]{0:T(1024)} %param.33) | copy-start | bytes 24580
  7.2 109.7 %all-gather.2.cloned.1.call-start = ((), (), s32[]{:S(2)}) async-start(), calls=%async_computation.2 | async-start | bytes 7798784 | tf_op jit(solution)/shard_map/all_gather | solution.py:103
  9.4 537.5 %reduce-scatter.5.cloned.1.call-start = ((), (), s32[]{:S(2)}) async-start(), calls=%async_computation.4 | async-start | bytes 4718592 | tf_op jit(solution)/shard_map/reduce_scatter | solution.py:277
  21.7 117.6 %copy-start.63 = (f32[768]{0:T(1024)}, f32[768]{0:T(1024)S(1)}, u32[]{:S(2)}) copy-start(f32[768]{0:T(1024)S(1)} %get-tuple-element.160) | copy-start | bytes 9220
  21.7 117.6 %copy-start.68 = (f32[768]{0:T(1024)}, f32[768]{0:T(1024)S(1)}, u32[]{:S(2)}) copy-start(f32[768]{0:T(1024)S(1)} %get-tuple-element.159) | copy-start | bytes 9220
  24.2 123.0 %copy-start.43 = (f32[2048,8]{0,1:T(8,128)}, f32[2048,8]{0,1:T(8,128)S(1)}, u32[]{:S(2)}) copy-start(f32[2048,8]{0,1:T(8,128)S(1)} %get-tuple-element.164) | copy-start | bytes 196612
  154.1 173.4 %copy-start.1 = (bf16[2048,6,64]{0,2,1:T(8,128)(2,1)}, bf16[2048,6,64]{0,2,1:T(8,128)(2,1)S(1)}, u32[]{:S(2)}) copy-start(bf16[2048,6,64]{0,2,1:T(8,128)(2,1)S(1)} %get-tuple-element.194) | copy-start | bytes 4718596
  264.9 35.5 %copy-start.7 = (f32[2048,6,64]{0,2,1:T(8,128)}, f32[2048,6,64]{0,2,1:T(8,128)S(1)}, u32[]{:S(2)}) copy-start(f32[2048,6,64]{0,2,1:T(8,128)S(1)} %fusion.46) | copy-start | bytes 9437188
  265.9 34.5 %copy-start.19 = (bf16[2048,768]{1,0:T(8,128)(2,1)S(1)}, bf16[2048,768]{1,0:T(8,128)(2,1)}, u32[]{:S(2)}) copy-start(bf16[2048,768]{1,0:T(8,128)(2,1)} %param.32) | copy-start | bytes 9437188
  265.9 34.5 %copy-start.38 = (bf16[12,6,128,128]{3,1,2,0:T(8,128)(2,1)S(1)}, bf16[12,6,128,128]{3,1,2,0:T(8,128)(2,1)}, u32[]{:S(2)}) copy-start(bf16[12,6,128,128]{3,1,2,0:T(8,128)(2,1)} %copy.45) | copy-start | bytes 7077892
  300.4 20.2 %copy-start.73 = (bf16[2048,1536]{1,0:T(8,128)(2,1)}, bf16[2048,1536]{1,0:T(8,128)(2,1)S(1)}, u32[]{:S(2)}) copy-start(bf16[2048,1536]{1,0:T(8,128)(2,1)S(1)} %get-tuple-element.170) | copy-start | bytes 18874372
  408.5 15.1 %slice-start.3 = ((s8[6291456]{0:T(1024)(128)(4,1)}), s8[4194304]{0:T(1024)(128)(4,1)S(1)}, s32[]{:S(2)}) async-start(s8[6291456]{0:T(1024)(128)(4,1)} %bitcast.232), calls=%async_computation.9 | async-start | bytes 8388608
  408.6 14.9 %copy-start.25 = (bf16[2048,6,64]{0,2,1:T(8,128)(2,1)}, bf16[2048,6,64]{0,2,1:T(8,128)(2,1)S(1)}, u32[]{:S(2)}) copy-start(bf16[2048,6,64]{0,2,1:T(8,128)(2,1)S(1)} %pad_maximum_fusion.4) | copy-start | bytes 4718596
  408.8 14.7 %copy-start.27 = (bf16[2048,6,64]{0,2,1:T(8,128)(2,1)}, bf16[2048,6,64]{0,2,1:T(8,128)(2,1)S(1)}, u32[]{:S(2)}) copy-start(bf16[2048,6,64]{0,2,1:T(8,128)(2,1)S(1)} %pad_maximum_fusion.5) | copy-start | bytes 4718596
  430.2 163.7 %reduce-scatter.3.cloned.1.call-start = ((), (), s32[]{:S(2)}) async-start(), calls=%async_computation.3 | async-start | bytes 4718592 | tf_op jit(solution)/shard_map/reduce_scatter | solution.py:198
  430.2 21.4 %slice-start.6 = ((s8[6291456]{0:T(1024)(128)(4,1)}), s8[4194304]{0:T(1024)(128)(4,1)S(1)}, s32[]{:S(2)}) async-start(s8[6291456]{0:T(1024)(128)(4,1)} %bitcast.274), calls=%async_computation.12 | async-start | bytes 8388608
  455.3 472.9 %all-reduce.4.cloned.1.call-start = ((), (), s32[]{:S(2)}) async-start(), calls=%async_computation.5 | async-start | bytes 28311552 | tf_op jit(solution)/shard_map/psum | solution.py:322
  542.3 51.6 %copy-start.61 = (f32[768]{0:T(1024)S(1)}, f32[768]{0:T(1024)}, u32[]{:S(2)}) copy-start(f32[768]{0:T(1024)} %get-tuple-element.156) | copy-start | bytes 9220
  542.3 51.7 %copy-start.62 = (f32[768]{0:T(1024)S(1)}, f32[768]{0:T(1024)}, u32[]{:S(2)}) copy-start(f32[768]{0:T(1024)} %get-tuple-element.161) | copy-start | bytes 9220
  546.9 51.1 %copy-start.55 = (f32[9984]{0:T(1024)S(1)}, f32[9984]{0:T(1024)}, u32[]{:S(2)}) copy-start(f32[9984]{0:T(1024)} %param.40) | copy-start | bytes 119812
  546.9 51.1 %copy-start.60 = (f32[9984]{0:T(1024)S(1)}, f32[9984]{0:T(1024)}, u32[]{:S(2)}) copy-start(f32[9984]{0:T(1024)} %param.41) | copy-start | bytes 119812
  598.0 346.4 %copy-start.30 = (f32[1,14,128,128]{3,2,1,0:T(8,128)S(1)}, f32[1,14,128,128]{3,2,1,0:T(8,128)}, u32[]{:S(2)}) copy-start(f32[1,14,128,128]{3,2,1,0:T(8,128)} %param.35) | copy-start | bytes 2752516
  (63 other events, 375.6 us)
Sparse Core Ops, SparseCore 0:
  11.3 105.5 all-gather.1
  430.3 9.4 reduce-scatter.4
  455.4 9.4 reduce-scatter.2
  536.8 391.3 all-reduce.3
where the time goes:
time: 962 us; the launch traced here: 953 us
  waiting for transfers between devices  419 us (44%)
  matrix products  267 us (28%)
  other arithmetic  119 us (12%)
  local copies, waits for them, and re-layouts  90.4 us (9%)
  blocking collectives  42.9 us (4%)
  between operations  15.6 us (2%)
    psum x1, waiting for transfers between devices, on_device(): summed = lax.psum(local_blocks, 'dp')  330 us
    all_gather x1, waiting for transfers between devices, on_device(): gathered = lax.all_gather(copies, 'dp', axis=0, tiled=True)  88.9 us
    dot_general x8, matrix products, contract(): lax.dot_general(first_op, second_op, (((first_dim,), (second_dim,)), ((),...  63.7 us
    psum x1, blocking collectives, on_device(): vector_sum = lax.psum(jnp.concatenate(pieces), ('dp', 'tensor'))  42.9 us
    convert_element_type x4, other arithmetic, on_device(): grad_scores = (prob_full * (grad_probs - row_delta)).astype(jnp.bfloat16)  39.5 us
    dot_general x4, matrix products, on_device(): jnp.einsum('qhe,khe->hqk', grad_attended[row_low:row_high], values_all[:r...  39.1 us
    dot_general x1, matrix products, on_device(): jnp.dot(norm_two, w_in, preferred_element_type=jnp.float32) + bias_in  34.4 us
    dot_general x4, matrix products, on_device(): jnp.einsum('hqk,qhe->khe', prob_low, grad_attended[row_low:row_high], pre...  27.2 us
  transfers between devices with their start and end apart: 4, of which 2 were waited for; matrix products, arithmetic and copies ran while one was open for 15% of the time, Pallas kernels for 0%

commit v1 on v0

--- a/solution.py
+++ b/solution.py
@@ -304,7 +304,9 @@
         ),
         bias_grad_out,
     ]
-    vector_sum = lax.psum(jnp.concatenate(pieces), ("dp", "tensor"))
+    block = jnp.concatenate(pieces)
+    shards = lax.all_gather(block, ("dp", "tensor"), axis=0, tiled=False)
+    vector_sum = shards.sum(axis=0)
     grad_scale = 1.0 / jnp.sqrt(jnp.float32(data_ways * tok_rows))
     vector_grad = vector_sum * grad_scale
     new_momentum = decay_vector * vector_momentum + (1.0 - decay_vector) * vector_grad

time: 962 us -> 998 us (1.037)
  waiting for transfers between devices: 419 us -> 494 us
  blocking collectives: 42.9 us -> 0 us
    psum x1, waiting for transfers between devices: 330 us -> 394 us  [on_device(): summed = lax.psum(local_blocks, 'dp')]
    psum x1 -> x0, blocking collectives: 42.9 us -> none  [on_device(): vector_sum = lax.psum(jnp.concatenate(pieces), ('dp', 'tensor'))]
    all_gather x0 -> x1, waiting for transfers between devices: none -> 10.7 us  [on_device(): shards = lax.all_gather(block, ('dp', 'tensor'), axis=0, tiled=False)]
  transfers between devices with their start and end apart: 4 -> 5, of which waited for: 2 -> 3; matrix products, arithmetic and copies ran while one was open for 15% -> 15% of each run, Pallas kernels for 0% -> 0%
where the time goes in v1:
time: 998 us; the launch traced here: 990 us
  waiting for transfers between devices  494 us (49%)
  matrix products  269 us (27%)
  other arithmetic  119 us (12%)
  local copies, waits for them, and re-layouts  91.8 us (9%)
  between operations  15.6 us (2%)
    psum x1, waiting for transfers between devices, on_device(): summed = lax.psum(local_blocks, 'dp')  394 us
    all_gather x1, waiting for transfers between devices, on_device(): gathered = lax.all_gather(copies, 'dp', axis=0, tiled=True)  88.8 us
    dot_general x8, matrix products, contract(): lax.dot_general(first_op, second_op, (((first_dim,), (second_dim,)), ((),...  65.9 us
    convert_element_type x4, other arithmetic, on_device(): grad_scores = (prob_full * (grad_probs - row_delta)).astype(jnp.bfloat16)  39.5 us
    dot_general x4, matrix products, on_device(): jnp.einsum('qhe,khe->hqk', grad_attended[row_low:row_high], values_all[:r...  39.2 us
    dot_general x1, matrix products, on_device(): jnp.dot(norm_two, w_in, preferred_element_type=jnp.float32) + bias_in  34.4 us
    dot_general x4, matrix products, on_device(): jnp.einsum('hqk,qhe->khe', prob_low, grad_attended[row_low:row_high], pre...  27.2 us
    dot_general x4, matrix products, on_device(): jnp.einsum('hqk,khe->qhe', weights_low, values_all[:key_span], preferred_...  26.5 us
  transfers between devices with their start and end apart: 5, of which 3 were waited for; matrix products, arithmetic and copies ran while one was open for 15% of the time, Pallas kernels for 0%

profile of v1, /device:TPU:0, one launch (start us, length us, event | category | flops | bytes accessed | tf_op | source)
XLA Modules:
  0.0 989.6 jit_solution(14693523701086706311)
XLA Ops:
  28.1 88.8 %all-gather.5.cloned.1.call-done = bf16[224,128,128]{2,1,0:T(8,128)(2,1)} async-done(((bf16[14,128,128]{2,1,0:T(8,128)(2,1)}), bf16[224,128,128]{2,1,0:T(8,128)(2,1)}) %all-gather.5.cloned.1.call-update) | async-done | bytes 7340048 | tf_op jit(solution)/shard_map/all_gather | solution.py:103
  116.9 11.4 %gather_fusion = bf16[216,128,128]{2,1,0:T(8,128)(2,1)} fusion(bf16[224,128,128]{2,1,0:T(8,128)(2,1)} %all-gather.5.cloned.1.call-done, s32[1024]{0:T(1024)S(1)} %pad_clamp_fusion.1), kind=kCustom, calls=%fused_computation | custom fusion | bytes 14156640 | tf_op jit(solution)/shard_map/jit(_take)/gather | solution.py:104
  194.5 7.3 multiply_convert_fusion.2
  206.2 8.3 fusion.161
  214.5 9.0 fusion.2
  223.6 10.5 %fusion.53 = f32[2048,6,64]{0,2,1:T(8,128)} fusion(f32[2048,6,64]{0,2,1:T(8,128)} %copy-done.7, bf16[512,6,64]{0,2,1:T(8,128)(2,1)S(1)} %bitcast.244, f32[6,512,1536]{2,1,0:T(8,128)} %get-tuple-element.177, f32[6,512]{1,0:T(8,128)S(1)} %log_add_fusion.1), kind=kOutput, calls=%fused_computation.109 | convolution fusion | flops 614006784 | bytes 23998464 | tf_op jit(solution)/shard_map/hqk,qhe->khe/dot_general | solution.py:254
  234.1 12.1 %multiply_reduce_fusion.1 = (f32[6,512]{1,0:T(8,128)S(1)}, f32[6,512,1536]{2,1,0:T(8,128)}) fusion(f32[6,512,1536]{2,1,0:T(8,128)} %get-tuple-element.177, f32[6,512]{1,0:T(8,128)S(1)} %log_add_fusion.1, bf16[512,6,64]{0,2,1:T(8,128)(2,1)S(1)} %bitcast.245, bf16[1536,6,64]{0,2,1:T(8,128)(2,1)S(1)} %bitcast.241), kind=kOutput, calls=%fused_computation.14 | convolution fusion | flops 618132480 | bytes 39346176 | tf_op jit(solution)/shard_map/qhe,khe->hqk/dot_general | solution.py:230
  246.2 12.9 %multiply_convert_fusion.1 = bf16[6,512,1536]{2,1,0:T(8,128)(2,1)S(1)} fusion(f32[6,512,1536]{2,1,0:T(8,128)} %get-tuple-element.187, f32[6,512,1536]{2,1,0:T(8,128)} %get-tuple-element.177, f32[6,512]{1,0:T(8,128)S(1)} %get-tuple-element.186, f32[6,512]{1,0:T(8,128)S(1)} %log_add_fusion.1), kind=kLoop, calls=%fused_computation.13 | loop fusion | flops 18874368 | bytes 47210496 | tf_op jit(solution)/shard_map/convert_element_type | solution.py:237
  265.9 34.4 %fusion.6 = (bf16[2048,1536]{1,0:T(8,128)(2,1)S(1)}, f32[2048,1536]{1,0:T(8,128)}) fusion(f32[1536]{0:T(1024)S(1)} %copy-done.65, bf16[96,8,12,128]{3,2,1,0:T(8,128)(2,1)S(1)} %bitcast.253, bf16[2048,768]{1,0:T(8,128)(2,1)S(1)} %copy-done.2, f32[768]{0:T(1024)S(1)} %copy-done.69, f32[768]{0:T(1024)S(1)} %copy-done.64, f32[2048]{0:T(1024)S(1)} %add_rsqrt_fusion, ...), kind=kOutput, calls=%fused_computation.24 | convolution fusion | flops 5048893440 | bytes 24408064 | tf_op jit(solution)/shard_map/dot_general | solution.py:191
  300.3 13.2 %convert_reduce_fusion = (f32[1536]{0:T(1024)}, bf16[2048,1536]{1,0:T(8,128)(2,1)S(1)}) fusion(f32[2048,1536]{1,0:T(8,128)} %get-tuple-element.171, f32[1536]{0:T(1024)S(1)} %copy-done.65, bf16[2048,768]{1,0:T(8,128)(2,1)S(1)} %copy-done.18, bf16[192,8,6,128]{3,2,1,0:T(8,128)(2,1)S(1)} %bitcast.255), kind=kOutput, calls=%fused_computation.32 | convolution fusion | flops 4872731136 | bytes 24391680 | tf_op jit(solution)/shard_map/dot_general | solution.py:18
  327.5 10.7 %fusion.160 = (f32[6,512]{1,0:T(8,128)S(1)}, f32[6,512,2048]{2,1,0:T(8,128)}) fusion(bf16[2048,6,64]{0,2,1:T(8,128)(2,1)S(1)} %get-tuple-element.194, bf16[2048,6,64]{0,2,1:T(8,128)(2,1)S(1)} %copy-done.12, pred[512,2048]{1,0:T(8,128)(4,1)S(1)} %copy-done.16), kind=kOutput, calls=%fused_computation.283 | convolution fusion | flops 824177664 | bytes 28192768 | tf_op jit(solution)/shard_map/qhe,khe->hqk/dot_general | solution.py:159
  338.2 10.9 %fusion = f32[6,512]{1,0:T(8,128)S(1)} fusion(f32[6,512,2048]{2,1,0:T(8,128)} %get-tuple-element.175, f32[6,512]{1,0:T(8,128)S(1)} %get-tuple-element.174), kind=kLoop, calls=%fused_computation.9 | loop fusion | flops 12579840 | bytes 25190400 | tf_op jit(solution)/shard_map/reduce_sum | solution.py:179
  349.1 11.9 %fusion.39 = bf16[2048,6,64]{0,2,1:T(8,128)(2,1)} fusion(f32[2048,6,64]{0,2,1:T(8,128)S(1)} %copy-done.8, bf16[512,6,64]{0,2,1:T(8,128)(2,1)S(1)} %bitcast.242, f32[6,512,2048]{2,1,0:T(8,128)} %get-tuple-element.175, f32[6,512]{1,0:T(8,128)S(1)} %log_add_fusion), kind=kOutput, calls=%fused_computation.97 | convolution fusion | flops 819462144 | bytes 30289920 | tf_op jit(solution)/shard_map/hqk,qhe->khe/dot_general | solution.py:254
  361.1 19.5 %multiply_reduce_fusion = (f32[6,512]{1,0:T(8,128)S(1)}, f32[6,512,2048]{2,1,0:T(8,128)}) fusion(f32[6,512,2048]{2,1,0:T(8,128)} %get-tuple-element.175, f32[6,512]{1,0:T(8,128)S(1)} %log_add_fusion, bf16[512,6,64]{0,2,1:T(8,128)(2,1)S(1)} %bitcast.243, bf16[2048,6,64]{0,2,1:T(8,128)(2,1)S(1)} %bitcast.227), kind=kOutput, calls=%fused_computation.4 | convolution fusion | flops 824177664 | bytes 52322304 | tf_op jit(solution)/shard_map/qhe,khe->hqk/dot_general | solution.py:230
  380.6 16.9 %multiply_convert_fusion = bf16[6,512,2048]{2,1,0:T(8,128)(2,1)S(1)} fusion(f32[6,512,2048]{2,1,0:T(8,128)} %get-tuple-element.189, f32[6,512,2048]{2,1,0:T(8,128)} %get-tuple-element.175, f32[6,512]{1,0:T(8,128)S(1)} %get-tuple-element.188, f32[6,512]{1,0:T(8,128)S(1)} %log_add_fusion), kind=kLoop, calls=%fused_computation.3 | loop fusion | flops 25165824 | bytes 62939136 | tf_op jit(solution)/shard_map/convert_element_type | solution.py:237
  412.1 11.4 %multiply_reduce_fusion.4 = (f32[768]{0:T(1024)S(1)}, f32[2048]{0:T(1024)S(1)}, f32[2048]{0:T(1024)S(1)}, f32[768]{0:T(1024)S(1)}, f32[768]{0:T(1024)S(1)}, /*in...) fusion(bf16[2048,768]{1,0:T(8,128)(2,1)S(1)} %copy-done.3, ...), kind=kOutput, calls=%fused_computation.67 | convolution fusion | flops 3664761856 | bytes 22284288 | tf_op jit(solution)/shard_map/dot_general | solution.py:18
  430.2 9.9 fusion.100
  440.1 10.7 %fusion.101 = bf16[6,64,512]{2,1,0:T(8,128)(2,1)S(1)} fusion(bf16[2048,6,64]{0,2,1:T(8,128)(2,1)S(1)} %bitcast.228, f32[6,512,2048]{2,1,0:T(8,128)} %get-tuple-element.175, f32[6,512]{1,0:T(8,128)S(1)} %fusion, f32[6,512]{1,0:T(8,128)S(1)} %get-tuple-element.174), kind=kOutput, calls=%fused_computation.170 | convolution fusion | flops 824377344 | bytes 27156480 | tf_op jit(solution)/shard_map/hqk,khe->qhe/dot_general | solution.py:182
  460.2 11.8 %fusion.153 = f32[768,1536]{1,0:T(8,128)} fusion(bf16[2048,1536]{1,0:T(8,128)(2,1)} %copy-done.73, bf16[2048,768]{1,0:T(8,128)(2,1)} %param.31, f32[768]{0:T(1024)S(1)} %copy-done.70, f32[768]{0:T(1024)S(1)} %copy-done.64, f32[2048]{0:T(1024)S(1)} %add_rsqrt_fusion, f32[2048]{0:T(1024)S(1)} %broadcast_multiply_fusion.4), kind=kOutput, calls=%fused_computation.276 | convolution fusion | flops 4841275392 | bytes 14178304 | tf_op jit(solution)/shard_map/dot_general | solution.py:18
  485.4 8.7 fusion.165
  514.5 8.8 fusion.152
  538.0 7.8 pad_maximum_fusion
  557.0 10.7 %all-gather.7.cloned.1.call-done = f32[32,1,9984]{2,1,0:T(1,128)} async-done(((f32[1,1,9984]{2,1,0:T(1,128)}), f32[32,1,9984]{2,1,0:T(1,128)}) %all-gather.7.cloned.1.call-update) | async-done | bytes 1277968 | tf_op jit(solution)/shard_map/all_gather | solution.py:308
  570.4 394.0 %all-reduce.4.cloned.1.call-done = f32[216,128,128]{2,1,0:T(8,128)} async-done(((f32[216,128,128]{2,1,0:T(8,128)}), f32[216,128,128]{2,1,0:T(8,128)}) %all-reduce.4.cloned.1.call-update) | async-done | bytes 14155792 | tf_op jit(solution)/shard_map/psum | solution.py:324
  (309 shorter events, 222.2 us)
Async XLA Ops:
  7.2 972.3 %copy-start = (f32[1,14,128,128]{3,2,1,0:T(8,128)S(1)}, f32[1,14,128,128]{3,2,1,0:T(8,128)}, u32[]{:S(2)}) copy-start(f32[1,14,128,128]{3,2,1,0:T(8,128)} %param.38) | copy-start | bytes 2752516
  7.2 14.9 %slice-start.5 = ((s32[2048]{0:T(1024)}), s32[1024]{0:T(1024)S(1)}, s32[]{:S(2)}) async-start(s32[2048]{0:T(1024)} %param.33), calls=%async_computation.12 | async-start | bytes 8192 | tf_op jit(solution)/shard_map/slice | solution.py:167
  7.2 17.1 %copy-start.52 = (s32[2048]{0:T(1024)S(1)}, s32[2048]{0:T(1024)}, u32[]{:S(2)}) copy-start(s32[2048]{0:T(1024)} %param.33) | copy-start | bytes 24580
  7.2 13.9 %copy-start.53 = (f32[9984]{0:T(1024)S(1)}, f32[9984]{0:T(1024)}, u32[]{:S(2)}) copy-start(f32[9984]{0:T(1024)} %param.40) | copy-start | bytes 119812
  7.2 109.7 %all-gather.5.cloned.1.call-start = ((), (), s32[]{:S(2)}) async-start(), calls=%async_computation.2 | async-start | bytes 7798784 | tf_op jit(solution)/shard_map/all_gather | solution.py:103
  9.4 500.4 %reduce-scatter.5.cloned.1.call-start = ((), (), s32[]{:S(2)}) async-start(), calls=%async_computation.4 | async-start | bytes 4718592 | tf_op jit(solution)/shard_map/reduce_scatter | solution.py:277
  21.8 117.6 %copy-start.62 = (f32[768]{0:T(1024)}, f32[768]{0:T(1024)S(1)}, u32[]{:S(2)}) copy-start(f32[768]{0:T(1024)S(1)} %get-tuple-element.160) | copy-start | bytes 9220
  21.8 117.6 %copy-start.67 = (f32[768]{0:T(1024)}, f32[768]{0:T(1024)S(1)}, u32[]{:S(2)}) copy-start(f32[768]{0:T(1024)S(1)} %get-tuple-element.159) | copy-start | bytes 9220
  24.3 122.9 %copy-start.40 = (f32[2048,8]{0,1:T(8,128)}, f32[2048,8]{0,1:T(8,128)S(1)}, u32[]{:S(2)}) copy-start(f32[2048,8]{0,1:T(8,128)S(1)} %get-tuple-element.164) | copy-start | bytes 196612
  154.2 173.3 %copy-start.1 = (bf16[2048,6,64]{0,2,1:T(8,128)(2,1)}, bf16[2048,6,64]{0,2,1:T(8,128)(2,1)S(1)}, u32[]{:S(2)}) copy-start(bf16[2048,6,64]{0,2,1:T(8,128)(2,1)S(1)} %get-tuple-element.194) | copy-start | bytes 4718596
  264.8 35.5 %copy-start.6 = (f32[2048,6,64]{0,2,1:T(8,128)}, f32[2048,6,64]{0,2,1:T(8,128)S(1)}, u32[]{:S(2)}) copy-start(f32[2048,6,64]{0,2,1:T(8,128)S(1)} %fusion.46) | copy-start | bytes 9437188
  265.8 34.5 %copy-start.18 = (bf16[2048,768]{1,0:T(8,128)(2,1)S(1)}, bf16[2048,768]{1,0:T(8,128)(2,1)}, u32[]{:S(2)}) copy-start(bf16[2048,768]{1,0:T(8,128)(2,1)} %param.32) | copy-start | bytes 9437188
  265.8 34.5 %copy-start.35 = (bf16[12,6,128,128]{3,1,2,0:T(8,128)(2,1)S(1)}, bf16[12,6,128,128]{3,1,2,0:T(8,128)(2,1)}, u32[]{:S(2)}) copy-start(bf16[12,6,128,128]{3,1,2,0:T(8,128)(2,1)} %copy.45) | copy-start | bytes 7077892
  300.3 20.2 %copy-start.72 = (bf16[2048,1536]{1,0:T(8,128)(2,1)}, bf16[2048,1536]{1,0:T(8,128)(2,1)S(1)}, u32[]{:S(2)}) copy-start(bf16[2048,1536]{1,0:T(8,128)(2,1)S(1)} %get-tuple-element.170) | copy-start | bytes 18874372
  408.4 15.1 %slice-start.3 = ((s8[6291456]{0:T(1024)(128)(4,1)}), s8[4194304]{0:T(1024)(128)(4,1)S(1)}, s32[]{:S(2)}) async-start(s8[6291456]{0:T(1024)(128)(4,1)} %bitcast.232), calls=%async_computation.10 | async-start | bytes 8388608
  408.6 14.8 %copy-start.24 = (bf16[2048,6,64]{0,2,1:T(8,128)(2,1)}, bf16[2048,6,64]{0,2,1:T(8,128)(2,1)S(1)}, u32[]{:S(2)}) copy-start(bf16[2048,6,64]{0,2,1:T(8,128)(2,1)S(1)} %pad_maximum_fusion.4) | copy-start | bytes 4718596
  408.8 14.7 %copy-start.25 = (bf16[2048,6,64]{0,2,1:T(8,128)(2,1)}, bf16[2048,6,64]{0,2,1:T(8,128)(2,1)S(1)}, u32[]{:S(2)}) copy-start(bf16[2048,6,64]{0,2,1:T(8,128)(2,1)S(1)} %pad_maximum_fusion.5) | copy-start | bytes 4718596
  430.1 122.6 %reduce-scatter.3.cloned.1.call-start = ((), (), s32[]{:S(2)}) async-start(), calls=%async_computation.3 | async-start | bytes 4718592 | tf_op jit(solution)/shard_map/reduce_scatter | solution.py:198
  430.2 21.4 %slice-start.6 = ((s8[6291456]{0:T(1024)(128)(4,1)}), s8[4194304]{0:T(1024)(128)(4,1)S(1)}, s32[]{:S(2)}) async-start(s8[6291456]{0:T(1024)(128)(4,1)} %bitcast.274), calls=%async_computation.13 | async-start | bytes 8388608
  455.2 112.5 %all-gather.7.cloned.1.call-start = ((), (), s32[]{:S(2)}) async-start(), calls=%async_computation.6 | async-start | bytes 1317888 | tf_op jit(solution)/shard_map/all_gather | solution.py:308
  514.5 449.9 %all-reduce.4.cloned.1.call-start = ((), (), s32[]{:S(2)}) async-start(), calls=%async_computation.5 | async-start | bytes 28311552 | tf_op jit(solution)/shard_map/psum | solution.py:324
  545.9 23.8 %copy-start.54 = (f32[9984]{0:T(1024)S(1)}, f32[9984]{0:T(1024)}, u32[]{:S(2)}) copy-start(f32[9984]{0:T(1024)} %param.40) | copy-start | bytes 119812
  545.9 23.8 %copy-start.59 = (f32[9984]{0:T(1024)S(1)}, f32[9984]{0:T(1024)}, u32[]{:S(2)}) copy-start(f32[9984]{0:T(1024)} %param.41) | copy-start | bytes 119812
  569.8 410.8 %copy-start.27 = (f32[1,14,128,128]{3,2,1,0:T(8,128)S(1)}, f32[1,14,128,128]{3,2,1,0:T(8,128)}, u32[]{:S(2)}) copy-start(f32[1,14,128,128]{3,2,1,0:T(8,128)} %param.35) | copy-start | bytes 2752516
  (63 other events, 376.7 us)
Sparse Core Ops, SparseCore 0:
  11.3 105.5 all-gather.4
  430.2 9.4 reduce-scatter.4
  455.3 9.4 reduce-scatter.2
  514.6 53.0 all-gather.6
  574.0 390.3 all-reduce.3
